TPU v7x, 256 devices: a whole 4x4x8 slice. The times are simulated.
256 devices in a mesh: dp: 16 (over y, x), section: 8 (over z), mp: 2 (over core).
Axes of the slice: x: 4, y: 4, z: 8, core: 2. Of those that a mesh axis runs over, the one named last changes fastest.
Arguments:
- hidden: bfloat16 [128, 32, 3072], P('dp', None, 'mp'), may hold values from -6 to 6
- lengths: int32 [128], P('dp'), may hold values from 1 to 32, as said below
- dest_group: int32 [128], P('dp'), may hold values from 0 to 15, as said below
- w_query: bfloat16 [8, 3072, 3072], P('section', 'dp', 'mp')
- w_keyval: bfloat16 [8, 3072, 2, 2, 128], P('section', None, 'mp')
- w_output: bfloat16 [8, 3072, 3072], P('section', 'dp', 'mp'), may hold values from -0.109375 to 0.109375
- norm_gain: float32 [8, 3072], P('section'), may hold values from 0.5 to 1.5
- norm_bias: float32 [8, 3072], P('section'), may hold values from -3 to 3
Outputs:
- final_rows: bfloat16 [256, 32, 3072], P(('dp', 'section'), None, 'mp')
Inputs may be any that keep to these rules, and one draw needn't show every extreme that they name: `lengths`: some file has exactly 32 tokens. `dest_group`: a quarter of the groups receive 16 files, a quarter 16 // 2 and the rest 16 // 4; at most 2 files of one source shard (its 8 files in a row) go to one group, and some shard sends exactly 2 to one group.
All inputs are finite; a program needn't handle non-finite values.
Results may differ from a plain program's by a relative error of at most 0.025.
Values may be sent and summed in bfloat16 or wider, within the bound.
A program may use at most 128 MiB of HBM per device.

v0:
```python
import jax
import jax.numpy as jnp
from jax import lax
from jax.sharding import PartitionSpec as P

HEADS = 24
KV_HEADS = 2
GSLOTS = 16


rope_base = 100000.0
norm_eps = 1e-05


def from_behind(value, axis, steps):
    count = lax.axis_size(axis)
    first, last = (max(0, -steps), min(count, count - steps))
    return lax.ppermute(value, axis, [(source, source + steps) for source in range(first, last)])


def rope_tables(length_n, head_size):
    position = jnp.arange(length_n).astype(jnp.float32)
    fraction = jnp.arange(head_size // 2).astype(jnp.float32) * (2.0 / head_size)
    inverse = jnp.power(jnp.float32(rope_base), -fraction)
    angles = position[:, None] * inverse[None, :]
    angles = jnp.concatenate([angles, angles], axis=-1)
    return (jnp.cos(angles), jnp.sin(angles))


def rotate_heads(values, cosine, sine):
    half_size = values.shape[-1] // 2
    turned = jnp.concatenate([-values[..., half_size:], values[..., :half_size]], axis=-1)
    return values * cosine + turned * sine


def layer_norm(stream, gain_row, bias_row):
    values = stream.astype(jnp.float32)
    center = jnp.mean(values, axis=-1, keepdims=True)
    spread = jnp.mean(jnp.square(values - center), axis=-1, keepdims=True)
    scaled = (values - center) * lax.rsqrt(spread + norm_eps)
    return (scaled * gain_row + bias_row).astype(jnp.bfloat16)


def per_device(hidden, lengths, dest_group, w_query, w_keyval, w_output, norm_gain, norm_bias):
    dp_count = lax.axis_size("dp")
    section_count = lax.axis_size("section")
    source_files, length_n, half_width = hidden.shape
    capacity = max(2, 4 * source_files // dp_count)
    order = jnp.arange(source_files)
    earlier = (dest_group[None, :] == dest_group[:, None]) & (order[None, :] < order[:, None])
    position = jnp.sum(earlier.astype(jnp.int32), axis=1)
    hits = (
        (dest_group[None, None, :] == jnp.arange(dp_count)[:, None, None])
        & (position[None, None, :] == jnp.arange(capacity)[None, :, None])
    ).astype(jnp.int32)
    chosen = jnp.sum(hits * order[None, None, :], axis=2)
    filled = jnp.sum(hits, axis=2)
    outgoing = jnp.take(hidden, chosen.reshape(-1), axis=0).reshape(
        dp_count, capacity, length_n, half_width
    )
    outgoing = jnp.where(filled[:, :, None, None] > 0, outgoing, jnp.zeros_like(outgoing))
    out_lengths = jnp.sum(hits * lengths[None, None, :], axis=2)
    arrived, arrived_len = (
        lax.all_to_all(outgoing, "dp", split_axis=0, concat_axis=0, tiled=True),
        lax.all_to_all(out_lengths, "dp", split_axis=0, concat_axis=0, tiled=True),
    )
    flat_len = arrived_len.reshape(-1)
    present = (flat_len > 0).astype(jnp.int32)
    ranking = jnp.cumsum(present) - 1
    select = ((ranking[None, :] == jnp.arange(GSLOTS)[:, None]) & (present[None, :] > 0)).astype(
        jnp.int32
    )
    source_pos = jnp.sum(select * jnp.arange(flat_len.shape[0])[None, :], axis=1)
    slot_len = jnp.sum(select * flat_len[None, :], axis=1)
    grouped = jnp.take(arrived.reshape(-1, length_n, half_width), source_pos, axis=0)
    grouped = jnp.where(slot_len[:, None, None] > 0, grouped, jnp.zeros_like(grouped))
    query_w, output_w = (
        lax.all_gather(w_query[0], "dp", axis=0, tiled=True),
        lax.all_gather(w_output[0], "dp", axis=0, tiled=True),
    )
    keyval_w = w_keyval[0]
    gain_row = norm_gain[0]
    bias_row = norm_bias[0]
    model_width = query_w.shape[0]
    local_kv = keyval_w.shape[1]
    head_size = keyval_w.shape[3]
    groups_n = HEADS // KV_HEADS
    cosine, sine = rope_tables(length_n, head_size)
    score_scale = head_size ** (-0.5)

    def compute(full_rows, file_lengths):
        files_n = full_rows.shape[0]
        normed = layer_norm(full_rows, gain_row, bias_row).reshape(files_n * length_n, model_width)
        query_all = jnp.dot(normed, query_w, preferred_element_type=jnp.float32)
        query_all = query_all.reshape(files_n, length_n, local_kv, groups_n, head_size)
        query_all = rotate_heads(
            query_all, cosine[None, :, None, None, :], sine[None, :, None, None, :]
        ).astype(jnp.bfloat16)
        keyval = jnp.dot(
            normed,
            keyval_w.reshape(model_width, local_kv * 2 * head_size),
            preferred_element_type=jnp.float32,
        )
        keyval = keyval.reshape(files_n, length_n, local_kv, 2, head_size)
        key_all = rotate_heads(
            keyval[:, :, :, 0, :], cosine[None, :, None, :], sine[None, :, None, :]
        ).astype(jnp.bfloat16)
        value_all = keyval[:, :, :, 1, :].astype(jnp.bfloat16)
        scores = (
            jnp.einsum("pikgh,pjkh->pkgij", query_all, key_all, preferred_element_type=jnp.float32)
            * score_scale
        )
        row_pos = jnp.arange(length_n)[:, None]
        col_pos = jnp.arange(length_n)[None, :]
        causal = (col_pos <= row_pos)[None, None, None, :, :]
        inside = col_pos[None, None, None, :, :] < file_lengths[:, None, None, None, None]
        scores = jnp.where(causal & inside, scores, -jnp.inf)
        highest = jnp.max(scores, axis=-1, keepdims=True)
        weights = jnp.exp(scores - highest)
        probs = (weights / jnp.sum(weights, axis=-1, keepdims=True)).astype(jnp.bfloat16)
        context = jnp.einsum(
            "pkgij,pjkh->pikgh", probs, value_all, preferred_element_type=jnp.float32
        )
        context = context.astype(jnp.bfloat16).reshape(
            files_n * length_n, local_kv * groups_n * head_size
        )
        partial_value = lax.dot_general(
            context, output_w, (((1,), (1,)), ((), ())), preferred_element_type=jnp.float32
        )
        return partial_value.reshape(files_n, length_n, model_width)

    per_micro = 2
    micro_count = GSLOTS // per_micro
    micro_rows = grouped.reshape(micro_count, per_micro, length_n, half_width)
    micro_len = slot_len.reshape(micro_count, per_micro)
    micro_live = jnp.max(micro_len, axis=1) > 0
    section_here = lax.axis_index("section")
    tick_count = micro_count + section_count - 1

    def advance(tick, carry):
        incoming, results = carry
        micro = tick - section_here
        inside_range = (micro >= 0) & (micro < micro_count)
        clipped = jnp.clip(micro, 0, micro_count - 1)
        fresh = lax.dynamic_index_in_dim(micro_rows, clipped, 0, keepdims=False)
        file_lengths = lax.dynamic_index_in_dim(micro_len, clipped, 0, keepdims=False)
        current = jnp.where(section_here == 0, fresh, incoming)
        full_rows = lax.all_gather(current, "mp", axis=2, tiled=True)
        active = inside_range & micro_live[clipped]
        partial_value = lax.cond(
            active,
            lambda: compute(full_rows, file_lengths),
            lambda: jnp.zeros((per_micro, length_n, model_width), jnp.float32),
        )
        reduced = lax.psum_scatter(
            partial_value.astype(jnp.bfloat16), "mp", scatter_dimension=2, tiled=True
        ).astype(jnp.float32)
        updated = (current.astype(jnp.float32) + reduced).astype(jnp.bfloat16)
        store = active & (section_here == section_count - 1)
        previous = lax.dynamic_index_in_dim(results, clipped, 0, keepdims=False)
        results = lax.dynamic_update_index_in_dim(
            results, jnp.where(store, updated, previous), clipped, 0
        )
        incoming = from_behind(updated, "section", 1)
        return (incoming, results)

    start = (
        jnp.zeros((per_micro, length_n, half_width), jnp.bfloat16),
        jnp.zeros((micro_count, per_micro, length_n, half_width), jnp.bfloat16),
    )
    incoming, results = lax.fori_loop(0, tick_count, advance, start)
    final = results.reshape(GSLOTS, length_n, half_width)
    keep = jnp.arange(length_n)[None, :] < slot_len[:, None]
    final = jnp.where(keep[:, :, None], final, jnp.zeros_like(final))
    collected = lax.psum_scatter(final, "section", scatter_dimension=0, tiled=True).astype(
        jnp.float32
    )
    return collected.astype(jnp.bfloat16)


def solution(mesh):
    in_specs = (
        P("dp", None, "mp"),
        P("dp"),
        P("dp"),
        P("section", "dp", "mp"),
        P("section", None, "mp", None, None),
        P("section", "dp", "mp"),
        P("section", None),
        P("section", None),
    )
    out_specs = P(("dp", "section"), None, "mp")
    return jax.shard_map(
        per_device, mesh=mesh, in_specs=in_specs, out_specs=out_specs, check_vma=False
    )
```

profile of v0, /device:TPU:6, one launch (start us, length us, event | category | flops | bytes accessed | tf_op | source)
XLA Modules:
  0.0 971.6 jit_solution(7053181556610693479)
XLA Ops:
  39.1 44.0 %all-to-all-done.1 = bf16[16,2,32,1536]{3,2,1,0:T(8,128)(2,1)} async-done(((bf16[16,2,32,1536]{3,2,1,0:T(8,128)(2,1)}), bf16[16,2,32,1536]{3,2,1,0:T(8,128)(2,1)}, u32[]{:S(2)}, u32[]{:S(2)}) %all-to-all-start.1) | async-done | bytes 3145760 | tf_op jit(solution)/shard_map/all_to_all | solution.py:64
  87.0 33.4 %all-gather.5.cloned.1.call-done = bf16[1,3072,1536]{2,1,0:T(8,128)(2,1)} async-done(((bf16[1,192,1536]{2,1,0:T(8,128)(2,1)}), bf16[1,3072,1536]{2,1,0:T(8,128)(2,1)}) %all-gather.5.cloned.1.call-update) | async-done | bytes 9437200 | tf_op jit(solution)/shard_map/all_gather | solution.py:78
  120.4 83.4 %all-gather.7.cloned.1.call-done = bf16[1,3072,1536]{2,1,0:T(8,128)(2,1)} async-done(((bf16[1,192,1536]{2,1,0:T(8,128)(2,1)}), bf16[1,3072,1536]{2,1,0:T(8,128)(2,1)}) %all-gather.7.cloned.1.call-update) | async-done | bytes 9437200 | tf_op jit(solution)/shard_map/all_gather | solution.py:79
  205.2 712.4 %while.16 = (s32[]{:T(128)}, bf16[2,32,1536]{2,1,0:T(8,128)(2,1)S(1)}, bf16[8,2,32,1536]{3,2,1,0:T(8,128)(2,1)}, pred[]{:T(512)}, s32[]{:T(128)}, /*index=5*/bf1...) while((s32[]{:T(128)}, ...), condition=%wide.region_16.17_spmd, body=%wide.region_8.16_spmd.sunk | while | flops 1325037184 | bytes 42566240 | solution.py:171
  209.6 19.0 %conditional.2 = (bf16[2,32,3072]{2,1,0:T(8,128)(2,1)S(1)}) conditional(s32[]{:T(128)} %convert_element_type.188, () %tuple.59, (bf16[2,32,3072]{2,1,0:T(8,128)(2,1)S(1)}, f32[1,3072]{1,0:T(1,128)S(1)}, f32[1,3072]{1,0:T(1,128)S(1)}, bf16[1,3072,1,2,128]{1,4,3,2,0:T(8,128)(2,1)}, s32[8,2]{1,0:T(8,128)}, /*index=5*/s32[]{:T(128)}, ...), branch_computations={%region_9.9_spmd, %region_10.14_spmd} | conditional | flops 1324447360 | bytes 35782108 | solution.py:150
  251.4 19.0 %conditional.2 = (bf16[2,32,3072]{2,1,0:T(8,128)(2,1)S(1)}) conditional(s32[]{:T(128)} %convert_element_type.188, () %tuple.59, (bf16[2,32,3072]{2,1,0:T(8,128)(2,1)S(1)}, f32[1,3072]{1,0:T(1,128)S(1)}, f32[1,3072]{1,0:T(1,128)S(1)}, bf16[1,3072,1,2,128]{1,4,3,2,0:T(8,128)(2,1)}, s32[8,2]{1,0:T(8,128)}, /*index=5*/s32[]{:T(128)}, ...), branch_computations={%region_9.9_spmd, %region_10.14_spmd} | conditional | flops 1324447360 | bytes 35782108 | solution.py:150
  296.7 19.0 %conditional.2 = (bf16[2,32,3072]{2,1,0:T(8,128)(2,1)S(1)}) conditional(s32[]{:T(128)} %convert_element_type.188, () %tuple.59, (bf16[2,32,3072]{2,1,0:T(8,128)(2,1)S(1)}, f32[1,3072]{1,0:T(1,128)S(1)}, f32[1,3072]{1,0:T(1,128)S(1)}, bf16[1,3072,1,2,128]{1,4,3,2,0:T(8,128)(2,1)}, s32[8,2]{1,0:T(8,128)}, /*index=5*/s32[]{:T(128)}, ...), branch_computations={%region_9.9_spmd, %region_10.14_spmd} | conditional | flops 1324447360 | bytes 35782108 | solution.py:150
  342.9 19.0 %conditional.2 = (bf16[2,32,3072]{2,1,0:T(8,128)(2,1)S(1)}) conditional(s32[]{:T(128)} %convert_element_type.188, () %tuple.59, (bf16[2,32,3072]{2,1,0:T(8,128)(2,1)S(1)}, f32[1,3072]{1,0:T(1,128)S(1)}, f32[1,3072]{1,0:T(1,128)S(1)}, bf16[1,3072,1,2,128]{1,4,3,2,0:T(8,128)(2,1)}, s32[8,2]{1,0:T(8,128)}, /*index=5*/s32[]{:T(128)}, ...), branch_computations={%region_9.9_spmd, %region_10.14_spmd} | conditional | flops 1324447360 | bytes 35782108 | solution.py:150
  390.4 19.0 %conditional.2 = (bf16[2,32,3072]{2,1,0:T(8,128)(2,1)S(1)}) conditional(s32[]{:T(128)} %convert_element_type.188, () %tuple.59, (bf16[2,32,3072]{2,1,0:T(8,128)(2,1)S(1)}, f32[1,3072]{1,0:T(1,128)S(1)}, f32[1,3072]{1,0:T(1,128)S(1)}, bf16[1,3072,1,2,128]{1,4,3,2,0:T(8,128)(2,1)}, s32[8,2]{1,0:T(8,128)}, /*index=5*/s32[]{:T(128)}, ...), branch_computations={%region_9.9_spmd, %region_10.14_spmd} | conditional | flops 1324447360 | bytes 35782108 | solution.py:150
  411.2 15.7 %reduce-scatter.5.cloned.1.call-done = bf16[2,32,1536]{2,1,0:T(8,128)(2,1)} async-done(((bf16[2,32,3072]{2,1,0:T(8,128)(2,1)}), bf16[2,32,1536]{2,1,0:T(8,128)(2,1)}) %reduce-scatter.5.cloned.1.call-update) | async-done | bytes 196624 | tf_op jit(solution)/shard_map/while/body/eval_jaxpr/reduce_scatter | solution.py:155
  441.1 19.0 %conditional.2 = (bf16[2,32,3072]{2,1,0:T(8,128)(2,1)S(1)}) conditional(s32[]{:T(128)} %convert_element_type.188, () %tuple.59, (bf16[2,32,3072]{2,1,0:T(8,128)(2,1)S(1)}, f32[1,3072]{1,0:T(1,128)S(1)}, f32[1,3072]{1,0:T(1,128)S(1)}, bf16[1,3072,1,2,128]{1,4,3,2,0:T(8,128)(2,1)}, s32[8,2]{1,0:T(8,128)}, /*index=5*/s32[]{:T(128)}, ...), branch_computations={%region_9.9_spmd, %region_10.14_spmd} | conditional | flops 1324447360 | bytes 35782108 | solution.py:150
  461.8 15.8 %reduce-scatter.5.cloned.1.call-done = bf16[2,32,1536]{2,1,0:T(8,128)(2,1)} async-done(((bf16[2,32,3072]{2,1,0:T(8,128)(2,1)}), bf16[2,32,1536]{2,1,0:T(8,128)(2,1)}) %reduce-scatter.5.cloned.1.call-update) | async-done | bytes 196624 | tf_op jit(solution)/shard_map/while/body/eval_jaxpr/reduce_scatter | solution.py:155
  491.8 19.0 %conditional.2 = (bf16[2,32,3072]{2,1,0:T(8,128)(2,1)S(1)}) conditional(s32[]{:T(128)} %convert_element_type.188, () %tuple.59, (bf16[2,32,3072]{2,1,0:T(8,128)(2,1)S(1)}, f32[1,3072]{1,0:T(1,128)S(1)}, f32[1,3072]{1,0:T(1,128)S(1)}, bf16[1,3072,1,2,128]{1,4,3,2,0:T(8,128)(2,1)}, s32[8,2]{1,0:T(8,128)}, /*index=5*/s32[]{:T(128)}, ...), branch_computations={%region_9.9_spmd, %region_10.14_spmd} | conditional | flops 1324447360 | bytes 35782108 | solution.py:150
  512.5 15.5 %reduce-scatter.5.cloned.1.call-done = bf16[2,32,1536]{2,1,0:T(8,128)(2,1)} async-done(((bf16[2,32,3072]{2,1,0:T(8,128)(2,1)}), bf16[2,32,1536]{2,1,0:T(8,128)(2,1)}) %reduce-scatter.5.cloned.1.call-update) | async-done | bytes 196624 | tf_op jit(solution)/shard_map/while/body/eval_jaxpr/reduce_scatter | solution.py:155
  542.2 19.0 %conditional.2 = (bf16[2,32,3072]{2,1,0:T(8,128)(2,1)S(1)}) conditional(s32[]{:T(128)} %convert_element_type.188, () %tuple.59, (bf16[2,32,3072]{2,1,0:T(8,128)(2,1)S(1)}, f32[1,3072]{1,0:T(1,128)S(1)}, f32[1,3072]{1,0:T(1,128)S(1)}, bf16[1,3072,1,2,128]{1,4,3,2,0:T(8,128)(2,1)}, s32[8,2]{1,0:T(8,128)}, /*index=5*/s32[]{:T(128)}, ...), branch_computations={%region_9.9_spmd, %region_10.14_spmd} | conditional | flops 1324447360 | bytes 35782108 | solution.py:150
  563.0 15.5 %reduce-scatter.5.cloned.1.call-done = bf16[2,32,1536]{2,1,0:T(8,128)(2,1)} async-done(((bf16[2,32,3072]{2,1,0:T(8,128)(2,1)}), bf16[2,32,1536]{2,1,0:T(8,128)(2,1)}) %reduce-scatter.5.cloned.1.call-update) | async-done | bytes 196624 | tf_op jit(solution)/shard_map/while/body/eval_jaxpr/reduce_scatter | solution.py:155
  594.4 32.4 %reduce-scatter.5.cloned.1.call-done = bf16[2,32,1536]{2,1,0:T(8,128)(2,1)} async-done(((bf16[2,32,3072]{2,1,0:T(8,128)(2,1)}), bf16[2,32,1536]{2,1,0:T(8,128)(2,1)}) %reduce-scatter.5.cloned.1.call-update) | async-done | bytes 196624 | tf_op jit(solution)/shard_map/while/body/eval_jaxpr/reduce_scatter | solution.py:155
  642.8 32.3 %reduce-scatter.5.cloned.1.call-done = bf16[2,32,1536]{2,1,0:T(8,128)(2,1)} async-done(((bf16[2,32,3072]{2,1,0:T(8,128)(2,1)}), bf16[2,32,1536]{2,1,0:T(8,128)(2,1)}) %reduce-scatter.5.cloned.1.call-update) | async-done | bytes 196624 | tf_op jit(solution)/shard_map/while/body/eval_jaxpr/reduce_scatter | solution.py:155
  691.0 32.3 %reduce-scatter.5.cloned.1.call-done = bf16[2,32,1536]{2,1,0:T(8,128)(2,1)} async-done(((bf16[2,32,3072]{2,1,0:T(8,128)(2,1)}), bf16[2,32,1536]{2,1,0:T(8,128)(2,1)}) %reduce-scatter.5.cloned.1.call-update) | async-done | bytes 196624 | tf_op jit(solution)/shard_map/while/body/eval_jaxpr/reduce_scatter | solution.py:155
  739.2 32.3 %reduce-scatter.5.cloned.1.call-done = bf16[2,32,1536]{2,1,0:T(8,128)(2,1)} async-done(((bf16[2,32,3072]{2,1,0:T(8,128)(2,1)}), bf16[2,32,1536]{2,1,0:T(8,128)(2,1)}) %reduce-scatter.5.cloned.1.call-update) | async-done | bytes 196624 | tf_op jit(solution)/shard_map/while/body/eval_jaxpr/reduce_scatter | solution.py:155
  787.4 30.3 %reduce-scatter.5.cloned.1.call-done = bf16[2,32,1536]{2,1,0:T(8,128)(2,1)} async-done(((bf16[2,32,3072]{2,1,0:T(8,128)(2,1)}), bf16[2,32,1536]{2,1,0:T(8,128)(2,1)}) %reduce-scatter.5.cloned.1.call-update) | async-done | bytes 196624 | tf_op jit(solution)/shard_map/while/body/eval_jaxpr/reduce_scatter | solution.py:155
  833.7 29.5 %reduce-scatter.5.cloned.1.call-done = bf16[2,32,1536]{2,1,0:T(8,128)(2,1)} async-done(((bf16[2,32,3072]{2,1,0:T(8,128)(2,1)}), bf16[2,32,1536]{2,1,0:T(8,128)(2,1)}) %reduce-scatter.5.cloned.1.call-update) | async-done | bytes 196624 | tf_op jit(solution)/shard_map/while/body/eval_jaxpr/reduce_scatter | solution.py:155
  879.1 28.6 %reduce-scatter.5.cloned.1.call-done = bf16[2,32,1536]{2,1,0:T(8,128)(2,1)} async-done(((bf16[2,32,3072]{2,1,0:T(8,128)(2,1)}), bf16[2,32,1536]{2,1,0:T(8,128)(2,1)}) %reduce-scatter.5.cloned.1.call-update) | async-done | bytes 196624 | tf_op jit(solution)/shard_map/while/body/eval_jaxpr/reduce_scatter | solution.py:155
  920.3 44.4 %reduce-scatter.3.cloned.1.call-done = bf16[2,32,1536]{2,1,0:T(8,128)(2,1)} async-done(((bf16[16,32,1536]{2,1,0:T(8,128)(2,1)}), bf16[2,32,1536]{2,1,0:T(8,128)(2,1)}) %reduce-scatter.3.cloned.1.call-update) | async-done | bytes 196624 | tf_op jit(solution)/shard_map/reduce_scatter | solution.py:175
  (578 shorter events, 461.0 us)
Async XLA Ops:
  6.5 113.9 %all-gather.5.cloned.1.call-start = ((), (), s32[]{:S(2)}) async-start(), calls=%async_computation.5 | async-start | bytes 10027008 | tf_op jit(solution)/shard_map/all_gather | solution.py:78
  7.3 196.6 %all-gather.7.cloned.1.call-start = ((), (), s32[]{:S(2)}) async-start(), calls=%async_computation.6 | async-start | bytes 10027008 | tf_op jit(solution)/shard_map/all_gather | solution.py:79
  11.1 14.2 %all-to-all-start = ((s32[16,1,2]{2,1,0:T(1,128)}), s32[16,1,2]{2,1,0:T(1,128)S(1)}, u32[]{:S(2)}, u32[]{:S(2)}) async-start(s32[16,1,2]{2,1,0:T(1,128)} %copy.33), calls=%async_computation.1 | async-start | bytes 16384 | tf_op jit(solution)/shard_map/all_to_all | solution.py:65
  25.3 57.7 %all-to-all-start.1 = ((bf16[16,2,32,1536]{3,2,1,0:T(8,128)(2,1)}), bf16[16,2,32,1536]{3,2,1,0:T(8,128)(2,1)}, u32[]{:S(2)}, u32[]{:S(2)}) async-start(bf16[16,2,32,1536]{3,2,1,0:T(8,128)(2,1)} %select_select_fusion), calls=%async_computation.2 | async-start | bytes 6291456 | tf_op jit(solution)/shard_map/all_to_all | solution.py:64
  205.2 32.0 %reduce-scatter.5.cloned.1.call-start = ((), (), s32[]{:S(2)}) async-start(), calls=%async_computation.7 | async-start | bytes 589824 | tf_op jit(solution)/shard_map/while/body/eval_jaxpr/reduce_scatter | solution.py:155
  247.0 35.5 %reduce-scatter.5.cloned.1.call-start = ((), (), s32[]{:S(2)}) async-start(), calls=%async_computation.7 | async-start | bytes 589824 | tf_op jit(solution)/shard_map/while/body/eval_jaxpr/reduce_scatter | solution.py:155
  284.2 8.1 collective-permute-start
  292.3 36.4 %reduce-scatter.5.cloned.1.call-start = ((), (), s32[]{:S(2)}) async-start(), calls=%async_computation.7 | async-start | bytes 589824 | tf_op jit(solution)/shard_map/while/body/eval_jaxpr/reduce_scatter | solution.py:155
  330.4 8.1 collective-permute-start
  338.5 37.7 %reduce-scatter.5.cloned.1.call-start = ((), (), s32[]{:S(2)}) async-start(), calls=%async_computation.7 | async-start | bytes 589824 | tf_op jit(solution)/shard_map/while/body/eval_jaxpr/reduce_scatter | solution.py:155
  377.9 8.1 collective-permute-start
  386.1 40.9 %reduce-scatter.5.cloned.1.call-start = ((), (), s32[]{:S(2)}) async-start(), calls=%async_computation.7 | async-start | bytes 589824 | tf_op jit(solution)/shard_map/while/body/eval_jaxpr/reduce_scatter | solution.py:155
  436.7 40.9 %reduce-scatter.5.cloned.1.call-start = ((), (), s32[]{:S(2)}) async-start(), calls=%async_computation.7 | async-start | bytes 589824 | tf_op jit(solution)/shard_map/while/body/eval_jaxpr/reduce_scatter | solution.py:155
  487.4 40.6 %reduce-scatter.5.cloned.1.call-start = ((), (), s32[]{:S(2)}) async-start(), calls=%async_computation.7 | async-start | bytes 589824 | tf_op jit(solution)/shard_map/while/body/eval_jaxpr/reduce_scatter | solution.py:155
  537.9 40.6 %reduce-scatter.5.cloned.1.call-start = ((), (), s32[]{:S(2)}) async-start(), calls=%async_computation.7 | async-start | bytes 589824 | tf_op jit(solution)/shard_map/while/body/eval_jaxpr/reduce_scatter | solution.py:155
  580.1 8.1 collective-permute-start
  588.3 38.5 %reduce-scatter.5.cloned.1.call-start = ((), (), s32[]{:S(2)}) async-start(), calls=%async_computation.7 | async-start | bytes 589824 | tf_op jit(solution)/shard_map/while/body/eval_jaxpr/reduce_scatter | solution.py:155
  636.6 38.4 %reduce-scatter.5.cloned.1.call-start = ((), (), s32[]{:S(2)}) async-start(), calls=%async_computation.7 | async-start | bytes 589824 | tf_op jit(solution)/shard_map/while/body/eval_jaxpr/reduce_scatter | solution.py:155
  684.8 38.4 %reduce-scatter.5.cloned.1.call-start = ((), (), s32[]{:S(2)}) async-start(), calls=%async_computation.7 | async-start | bytes 589824 | tf_op jit(solution)/shard_map/while/body/eval_jaxpr/reduce_scatter | solution.py:155
  733.1 38.4 %reduce-scatter.5.cloned.1.call-start = ((), (), s32[]{:S(2)}) async-start(), calls=%async_computation.7 | async-start | bytes 589824 | tf_op jit(solution)/shard_map/while/body/eval_jaxpr/reduce_scatter | solution.py:155
  781.3 36.4 %reduce-scatter.5.cloned.1.call-start = ((), (), s32[]{:S(2)}) async-start(), calls=%async_computation.7 | async-start | bytes 589824 | tf_op jit(solution)/shard_map/while/body/eval_jaxpr/reduce_scatter | solution.py:155
  827.5 35.6 %reduce-scatter.5.cloned.1.call-start = ((), (), s32[]{:S(2)}) async-start(), calls=%async_computation.7 | async-start | bytes 589824 | tf_op jit(solution)/shard_map/while/body/eval_jaxpr/reduce_scatter | solution.py:155
  872.9 34.8 %reduce-scatter.5.cloned.1.call-start = ((), (), s32[]{:S(2)}) async-start(), calls=%async_computation.7 | async-start | bytes 589824 | tf_op jit(solution)/shard_map/while/body/eval_jaxpr/reduce_scatter | solution.py:155
  917.5 47.2 %reduce-scatter.3.cloned.1.call-start = ((), (), s32[]{:S(2)}) async-start(), calls=%async_computation.4 | async-start | bytes 1769472 | tf_op jit(solution)/shard_map/reduce_scatter | solution.py:175
  (107 other events, 1984.2 us)
Sparse Core Ops, SparseCore 0:
  9.8 110.6 all-gather.4
  122.9 80.9 all-gather.6
  229.5 7.6 reduce-scatter.4
  271.3 11.1 reduce-scatter.4
  316.6 12.1 reduce-scatter.4
  362.8 13.3 reduce-scatter.4
  410.4 16.5 reduce-scatter.4
  461.0 16.5 reduce-scatter.4
  511.7 16.2 reduce-scatter.4
  562.1 16.2 reduce-scatter.4
  593.6 33.1 reduce-scatter.4
  641.9 33.0 reduce-scatter.4
  690.1 33.0 reduce-scatter.4
  738.4 33.0 reduce-scatter.4
  786.6 31.0 reduce-scatter.4
  832.8 30.2 reduce-scatter.4
  878.3 29.4 reduce-scatter.4
  920.6 44.1 reduce-scatter.2
where the time goes:
time: 975 us; the launch traced here: 972 us
  waiting for transfers between devices  598 us (61%)
  matrix products  107 us (11%)
  other arithmetic  82.2 us (8%)
  starting transfers between devices  67.5 us (7%)
  local copies, waits for them, and re-layouts  60.7 us (6%)
  blocking collectives  31.3 us (3%)
  between operations  13.5 us (1%)
  loops' own time  12.2 us (1%)
    reduce_scatter x15, waiting for transfers between devices, advance(): lax.psum_scatter(partial_value.astype(jnp.bfloat16), 'mp', scatter_dimens...  321 us
    all_gather x1, waiting for transfers between devices, per_device(): lax.all_gather(w_output[0], 'dp', axis=0, tiled=True)  83.4 us
    ppermute x15, waiting for transfers between devices, from_behind(): lax.ppermute(value, axis, [(source, source + steps) for source in range(f...  69.6 us
    dot_general x8, matrix products, compute(): lax.dot_general(context, output_w, (((1,), (1,)), ((), ())), preferred_el...  52.9 us
    ppermute x15, starting transfers between devices, from_behind(): lax.ppermute(value, axis, [(source, source + steps) for source in range(f...  52 us
    reduce_scatter x1, waiting for transfers between devices, per_device(): lax.psum_scatter(final, 'section', scatter_dimension=0, tiled=True)  44.4 us
    all_to_all x1, waiting for transfers between devices, per_device(): lax.all_to_all(outgoing, 'dp', split_axis=0, concat_axis=0, tiled=True)  44 us
    dot_general x8, matrix products, compute(): query_all = jnp.dot(normed, query_w, preferred_element_type=jnp.float32)  43 us
  transfers between devices with their start and end apart: 35, of which 34 were waited for; matrix products, arithmetic and copies ran while one was open for 4% of the time, Pallas kernels for 0%

commit v1 on v0

v1 whole, which is shorter than its diff:
```python
import functools

import jax
import jax.numpy as jnp
from jax import lax
from jax.experimental import pallas as pl
from jax.experimental.pallas import tpu as pltpu
from jax.sharding import PartitionSpec as P

GSLOTS = 16
MESH = pl.DeviceIdType.MESH

rope_base = 100000.0
norm_eps = 1e-05

FILES_N = 8
LEN = 32
ROWS = FILES_N * LEN
WIDTH = 3072
HALF = 1536
SHARD = 192
PART = 48
HEAD = 128
GROUP = 12
MICRO = 64
MICROS = ROWS // MICRO
MFILES = MICRO // LEN
SECTIONS = 8
SIDE = 4
CUT = 384


def rope_tables(length_n, head_size):
    position = jnp.arange(length_n).astype(jnp.float32)
    fraction = jnp.arange(head_size // 2).astype(jnp.float32) * (2.0 / head_size)
    inverse = jnp.power(jnp.float32(rope_base), -fraction)
    angles = position[:, None] * inverse[None, :]
    cosine, sine = jnp.cos(angles), jnp.sin(angles)
    return (
        jnp.concatenate([cosine, cosine], axis=-1),
        jnp.concatenate([-sine, sine], axis=-1),
    )


def layer_pipeline(
    hidden, wq_own, wo_own, wkv_hbm, gain, bias, cosine, sine, keyok, rowok, out,
    wq, wo, wkv, stream, psend, precv, updated, final, piece, normed, queries, context,
    local_sem, gsend, grecv, zsend, zrecv, asend, arecv, rsend, rrecv, ssend, srecv,
):
    dp = lax.axis_index("dp")
    section = lax.axis_index("section")
    core = lax.axis_index("mp")
    x = lax.rem(dp, SIDE)
    y = dp // SIDE

    def at_xy(xx, yy):
        return lax.rem(yy + SIDE, SIDE) * SIDE + lax.rem(xx + SIDE, SIDE)

    other = 1 - core
    partner = (dp, section, other)
    steps = ((1, 0), (-1, 0), (0, 1), (0, -1))

    barrier = pltpu.get_barrier_semaphore()
    for sx, sy in steps:
        pl.semaphore_signal(
            barrier, inc=1, device_id=(at_xy(x + sx, y + sy), section, core), device_id_type=MESH
        )
    pl.semaphore_signal(barrier, inc=1, device_id=partner, device_id_type=MESH)
    for k in range(1, SECTIONS):
        pl.semaphore_signal(
            barrier, inc=1, device_id=(dp, lax.rem(section + k, SECTIONS), core), device_id_type=MESH
        )
    pl.semaphore_wait(barrier, 4 + 1 + SECTIONS - 1)

    own_cols = pl.ds(pl.multiple_of(core * HALF, HALF), HALF)

    copies = [
        pltpu.make_async_copy(wq_own, wq.at[pl.ds(pl.multiple_of(dp * SHARD, SHARD), SHARD), :], local_sem.at[0]),
        pltpu.make_async_copy(wo_own, wo.at[pl.ds(pl.multiple_of(dp * SHARD, SHARD), SHARD), :], local_sem.at[1]),
        pltpu.make_async_copy(wkv_hbm, wkv, local_sem.at[2]),
    ]
    for copy in copies:
        copy.start()

    def rows_of(source, part):
        return pl.ds(pl.multiple_of(source * SHARD + part * PART, PART), PART)

    def push(w, source, part, direction, own):
        full = (wq, wo)[w]
        sx, sy = steps[direction]
        place = full.at[rows_of(source, part), :]
        src = (wq_own, wo_own)[w].at[pl.ds(part * PART, PART), :] if own else place
        pltpu.make_async_remote_copy(
            src_ref=src,
            dst_ref=place,
            send_sem=gsend.at[w, direction],
            recv_sem=grecv.at[w, source, part],
            device_id=(at_xy(x + sx, y + sy), section, core),
            device_id_type=MESH,
        ).start()

    def arrived(w, source, part):
        place = (wq, wo)[w].at[rows_of(source, part), :]
        pltpu.make_async_copy(place, place, grecv.at[w, source, part]).wait()

    def first_dirs(colour):
        return (0, 1) if colour == 0 else (2, 3)

    def second_dirs(colour):
        return (2, 3) if colour == 0 else (0, 1)

    def along(colour, k):
        return at_xy(x + k, y) if colour == 0 else at_xy(x, y + k)

    def across(colour, k, j):
        return at_xy(x + k, y + j) if colour == 0 else at_xy(x + j, y + k)

    def spread_own(w):
        for dirs in (first_dirs, second_dirs):
            for part in range(2):
                for colour in range(2):
                    for direction in dirs(colour):
                        push(w, dp, 2 * colour + part, direction, True)

    def relay_first(w):
        for part in range(2):
            for colour in range(2):
                forward, backward = first_dirs(colour)
                arrived(w, along(colour, -1), 2 * colour + part)
                if part == 0:
                    push(w, along(colour, -1), 2 * colour, forward, False)
                arrived(w, along(colour, 1), 2 * colour + part)
                if part == 1:
                    push(w, along(colour, 1), 2 * colour + 1, backward, False)
        for k in (-1, 1):
            for part in range(2):
                for colour in range(2):
                    for direction in second_dirs(colour):
                        push(w, along(colour, k), 2 * colour + part, direction, False)

    def relay_opposite(w):
        for part in range(2):
            for colour in range(2):
                arrived(w, along(colour, 2), 2 * colour + part)
                for direction in second_dirs(colour):
                    push(w, along(colour, 2), 2 * colour + part, direction, False)

    def relay_second(w, k):
        for part in range(2):
            for colour in range(2):
                forward, backward = second_dirs(colour)
                arrived(w, across(colour, k, -1), 2 * colour + part)
                if part == 0:
                    push(w, across(colour, k, -1), 2 * colour, forward, False)
                arrived(w, across(colour, k, 1), 2 * colour + part)
                if part == 1:
                    push(w, across(colour, k, 1), 2 * colour + 1, backward, False)

    def finish(w):
        for k in (0, -1, 1, 2):
            for part in range(2):
                for colour in range(2):
                    arrived(w, across(colour, k, 2), 2 * colour + part)

    spread_own(0)
    relay_first(0)
    spread_own(1)
    relay_opposite(0)
    relay_second(0, 0)
    relay_first(1)
    relay_second(0, -1)
    relay_second(0, 1)
    relay_opposite(1)
    relay_second(0, 2)
    finish(0)
    for k in (0, -1, 1, 2):
        relay_second(1, k)
    finish(1)
    for w in range(2):
        for direction in range(4):
            sent = (wq, wo)[w].at[pl.ds(0, 15 * PART), :]
            pltpu.make_async_copy(sent, sent, gsend.at[w, direction]).wait()
    for copy in copies:
        copy.wait()

    @pl.when(section == 0)
    def _():
        first = pltpu.make_async_copy(hidden, stream.at[:, own_cols], local_sem.at[3])
        first.start()
        first.wait()

    row_id = lax.broadcasted_iota(jnp.int32, (MICRO, MICRO), 0)
    col_id = lax.broadcasted_iota(jnp.int32, (MICRO, MICRO), 1)
    causal = (row_id // LEN == col_id // LEN) & (col_id <= row_id)

    def micro_rows(i):
        return pl.ds(pl.multiple_of(i * MICRO, MICRO), MICRO)

    def hop(i, to_section):
        rows = micro_rows(i)
        return pltpu.make_async_remote_copy(
            src_ref=updated.at[rows, :],
            dst_ref=stream.at[rows, own_cols],
            send_sem=zsend.at[i],
            recv_sem=zrecv.at[i],
            device_id=(dp, to_section, core),
            device_id_type=MESH,
        )

    def swap(i):
        rows = micro_rows(i)
        return pltpu.make_async_remote_copy(
            src_ref=stream.at[rows, own_cols],
            dst_ref=stream.at[rows, own_cols],
            send_sem=asend.at[i],
            recv_sem=arecv.at[i],
            device_id=partner,
            device_id_type=MESH,
        )

    def give(i):
        rows = micro_rows(i)
        return pltpu.make_async_remote_copy(
            src_ref=psend.at[rows, :],
            dst_ref=precv.at[rows, :],
            send_sem=rsend.at[i],
            recv_sem=rrecv.at[i],
            device_id=partner,
            device_id_type=MESH,
        )

    def spread(i, target):
        files = pl.ds(i * MFILES, MFILES)
        return (
            final.at[files, target // 4, :, pl.ds((target % 4) * CUT, CUT)],
            piece.at[files, :, :],
        )

    score_scale = HEAD ** (-0.5)

    def step(i, carry):
        rows = micro_rows(i)

        @pl.when(section > 0)
        def _():
            hop(i, section).wait_recv()

        exchange = swap(i)
        exchange.start()
        exchange.wait_recv()

        for block in range(MICRO // 16):
            part = pl.ds(pl.multiple_of(i * MICRO + block * 16, 16), 16)
            values = stream[part, :].astype(jnp.float32)
            center = jnp.mean(values, axis=-1, keepdims=True)
            values = values - center
            variance = jnp.mean(values * values, axis=-1, keepdims=True)
            scaled = values * lax.rsqrt(variance + norm_eps)
            normed[block * 16 : (block + 1) * 16, :] = (scaled * gain[...] + bias[...]).astype(
                jnp.bfloat16
            )

        cos_t = cosine[...]
        sin_t = sine[...]

        def rotate(values):
            return values * cos_t + pltpu.roll(values, HEAD // 2, 1) * sin_t

        keyval = jnp.dot(normed[...], wkv[...], preferred_element_type=jnp.float32)
        key = rotate(keyval[:, :HEAD]).astype(jnp.bfloat16)
        value = keyval[:, HEAD:].astype(jnp.bfloat16)
        for j in range(GROUP // 2):
            pair = jnp.dot(
                normed[...], wq[:, j * 256 : (j + 1) * 256], preferred_element_type=jnp.float32
            )
            for k in range(2):
                h = 2 * j + k
                queries[h * MICRO : (h + 1) * MICRO, :] = rotate(
                    pair[:, k * HEAD : (k + 1) * HEAD]
                ).astype(jnp.bfloat16)
        scores = lax.dot_general(
            queries[...], key, (((1,), (1,)), ((), ())), preferred_element_type=jnp.float32
        )
        ok = causal & (keyok[pl.ds(pl.multiple_of(i * 8, 8), 8), :][0:1, :] > 0.5)
        scores = (scores * score_scale).reshape(GROUP, MICRO, MICRO)
        scores = jnp.where(ok[None], scores, -jnp.inf)
        highest = jnp.max(scores, axis=-1, keepdims=True)
        weights = jnp.exp(scores - highest)
        total = jnp.sum(weights, axis=-1, keepdims=True)
        probs = (weights / total).astype(jnp.bfloat16).reshape(GROUP * MICRO, MICRO)
        mixed = jnp.dot(probs, value, preferred_element_type=jnp.float32).astype(jnp.bfloat16)
        for h in range(GROUP):
            context[:, h * HEAD : (h + 1) * HEAD] = mixed[h * MICRO : (h + 1) * MICRO, :]

        def project(half, j):
            start = pl.multiple_of(half * HALF + j * 256, 256)
            return lax.dot_general(
                context[...],
                wo[pl.ds(start, 256), :],
                (((1,), (1,)), ((), ())),
                preferred_element_type=jnp.float32,
            ).astype(jnp.bfloat16)

        for j in range(HALF // 256):
            psend[rows, j * 256 : (j + 1) * 256] = project(other, j)
        handed = give(i)
        handed.start()
        for j in range(HALF // 256):
            updated[rows, j * 256 : (j + 1) * 256] = project(core, j)
        handed.wait_recv()
        mine = updated[rows, :].astype(jnp.float32) + precv[rows, :].astype(jnp.float32)
        result = (stream[rows, own_cols].astype(jnp.float32) + mine).astype(jnp.bfloat16)
        updated[rows, :] = result

        @pl.when(section < SECTIONS - 1)
        def _():
            hop(i, section + 1).start()

        @pl.when(section == SECTIONS - 1)
        def _():
            kept = jnp.where(rowok[rows, :][:, 0:1] > 0.5, result, jnp.zeros_like(result))
            final[pl.ds(i * MFILES, MFILES)] = kept.reshape(MFILES, 2, 16, HALF)
            for target in range(SECTIONS - 1):
                src, dst = spread(i, target)
                pltpu.make_async_remote_copy(
                    src_ref=src,
                    dst_ref=dst,
                    send_sem=ssend.at[i, target],
                    recv_sem=srecv.at[i],
                    device_id=(dp, target, core),
                    device_id_type=MESH,
                ).start()
            src, dst = spread(i, SECTIONS - 1)
            pltpu.make_async_copy(src, dst, srecv.at[i]).start()

        return carry

    lax.fori_loop(0, MICROS, step, 0)

    def drain(i, carry):
        swap(i).wait_send()
        give(i).wait_send()

        @pl.when(section < SECTIONS - 1)
        def _():
            hop(i, section).wait_send()

        @pl.when(section == SECTIONS - 1)
        def _():
            for target in range(SECTIONS - 1):
                src, dst = spread(i, target)
                pltpu.make_async_copy(src, dst, ssend.at[i, target]).wait()

        files = piece.at[pl.ds(i * MFILES, MFILES), :, :]
        pltpu.make_async_copy(files, files, srecv.at[i]).wait()
        return carry

    lax.fori_loop(0, MICROS, drain, 0)
    out[...] = piece[...]


def per_device(hidden, lengths, dest_group, w_query, w_keyval, w_output, norm_gain, norm_bias):
    dp_count = lax.axis_size("dp")
    section_count = lax.axis_size("section")
    source_files, length_n, half_width = hidden.shape
    capacity = 2
    order = jnp.arange(source_files)
    earlier = (dest_group[None, :] == dest_group[:, None]) & (order[None, :] < order[:, None])
    position = jnp.sum(earlier.astype(jnp.int32), axis=1)
    hits = (
        (dest_group[None, None, :] == jnp.arange(dp_count)[:, None, None])
        & (position[None, None, :] == jnp.arange(capacity)[None, :, None])
    ).astype(jnp.int32)
    filled = jnp.sum(hits, axis=2)
    arrived_filled = lax.all_to_all(filled, "dp", split_axis=0, concat_axis=0, tiled=True)
    present = arrived_filled.reshape(-1)
    ranking = jnp.cumsum(present) - 1
    select = ((ranking[None, :] == jnp.arange(GSLOTS)[:, None]) & (present[None, :] > 0)).astype(
        jnp.bfloat16
    )

    inside = (jnp.arange(length_n)[None, :] < lengths[:, None]).astype(jnp.float32)
    keyok = jnp.broadcast_to(inside.reshape(MICROS, 1, MICRO), (MICROS, 8, MICRO)).reshape(
        MICROS * 8, MICRO
    )
    rowok = jnp.broadcast_to(inside.reshape(ROWS, 1), (ROWS, 128))
    cosine, sine = rope_tables(length_n, HEAD)
    cosine, sine = jnp.tile(cosine, (MFILES, 1)), jnp.tile(sine, (MFILES, 1))

    anywhere = pl.BlockSpec(memory_space=pl.ANY)
    inner = pl.BlockSpec(memory_space=pltpu.VMEM)
    dma = pltpu.SemaphoreType.DMA
    bf16 = jnp.bfloat16
    pieces = pl.pallas_call(
        layer_pipeline,
        out_shape=jax.ShapeDtypeStruct((FILES_N, 16, CUT), bf16),
        in_specs=[anywhere] * 4 + [inner] * 6,
        out_specs=inner,
        scratch_shapes=[
            pltpu.VMEM((WIDTH, HALF), bf16),
            pltpu.VMEM((WIDTH, HALF), bf16),
            pltpu.VMEM((WIDTH, 2 * HEAD), bf16),
            pltpu.VMEM((ROWS, WIDTH), bf16),
            pltpu.VMEM((ROWS, HALF), bf16),
            pltpu.VMEM((ROWS, HALF), bf16),
            pltpu.VMEM((ROWS, HALF), bf16),
            pltpu.VMEM((FILES_N, 2, 16, HALF), bf16),
            pltpu.VMEM((FILES_N, 16, CUT), bf16),
            pltpu.VMEM((MICRO, WIDTH), bf16),
            pltpu.VMEM((GROUP * MICRO, HEAD), bf16),
            pltpu.VMEM((MICRO, HALF), bf16),
            dma((4,)),
            dma((2, 4)),
            dma((2, 16, 4)),
            dma((MICROS,)),
            dma((MICROS,)),
            dma((MICROS,)),
            dma((MICROS,)),
            dma((MICROS,)),
            dma((MICROS,)),
            dma((MICROS, SECTIONS)),
            dma((MICROS,)),
        ],
        compiler_params=pltpu.CompilerParams(
            collective_id=0, has_side_effects=True, vmem_limit_bytes=56 * 2**20
        ),
        name="layers",
    )(
        hidden.reshape(ROWS, HALF),
        w_query[0],
        w_output[0],
        w_keyval[0].reshape(WIDTH, 2 * HEAD),
        norm_gain,
        norm_bias,
        cosine,
        sine,
        keyok,
        rowok,
    )
    flat = pieces.reshape(source_files, 16 * CUT)
    outgoing = jnp.dot(
        hits.reshape(dp_count * capacity, source_files).astype(bf16),
        flat,
        preferred_element_type=bf16,
    ).reshape(dp_count, capacity, 16 * CUT)
    arrived = lax.all_to_all(outgoing, "dp", split_axis=0, concat_axis=0, tiled=True)
    slots = jnp.dot(
        select, arrived.reshape(dp_count * capacity, 16 * CUT), preferred_element_type=bf16
    ).reshape(section_count, GSLOTS // section_count, 16 * CUT)
    mine = lax.all_to_all(slots, "section", split_axis=0, concat_axis=0, tiled=True)
    mine = mine.reshape(2, 4, 2, 16, CUT).transpose(2, 0, 3, 1, 4)
    return mine.reshape(GSLOTS // section_count, length_n, half_width)


def solution(mesh):
    in_specs = (
        P("dp", None, "mp"),
        P("dp"),
        P("dp"),
        P("section", "dp", "mp"),
        P("section", None, "mp", None, None),
        P("section", "dp", "mp"),
        P("section", None),
        P("section", None),
    )
    out_specs = P(("dp", "section"), None, "mp")
    return jax.shard_map(
        per_device, mesh=mesh, in_specs=in_specs, out_specs=out_specs, check_vma=False
    )
```

time: 975 us -> 290 us (0.30)
  waiting for transfers between devices: 598 us -> 5.25 us
  Pallas kernels: 0 us -> 239 us
  matrix products: 107 us -> 0.61 us
  other arithmetic: 82.2 us -> 3.58 us
  starting transfers between devices: 67.5 us -> 14.1 us
  local copies, waits for them, and re-layouts: 60.7 us -> 11.2 us
  blocking collectives: 31.3 us -> 14.7 us
  between operations: 13.5 us -> 0.09 us
  loops' own time: 12.2 us -> 0 us
    reduce_scatter x16 -> x0, waiting for transfers between devices: 366 us -> none  [the longest x15 321 us: advance(): lax.psum_scatter(partial_value.astype(jnp.bfloat16), 'mp', scatter_dimens...]
    pallas_call x0 -> x1, Pallas kernels: none -> 239 us  [per_device(): pl.pallas_call(layer_pipeline, out_shape=jax.ShapeDtypeStruct((FILES_N, 1...]
    all_gather x2 -> x0, waiting for transfers between devices: 117 us -> none  [the longest x1 83.4 us: per_device(): lax.all_gather(w_output[0], 'dp', axis=0, tiled=True)]
    dot_general x40 -> x2, matrix products: 107 us -> 0.61 us  [the longest x1 0.36 us: per_device(): jnp.dot(hits.reshape(dp_count * capacity, source_files).astype(bf16), fla...]
    ppermute x15 -> x0, waiting for transfers between devices: 69.6 us -> none  [from_behind(): lax.ppermute(value, axis, [(source, source + steps) for source in range(f...]
    ppermute x15 -> x0, starting transfers between devices: 52 us -> none  [from_behind(): lax.ppermute(value, axis, [(source, source + steps) for source in range(f...]
    all_to_all x1, waiting for transfers between devices: 44 us -> 5.25 us  [per_device(): lax.all_to_all(outgoing, 'dp', split_axis=0, concat_axis=0, tiled=True)]
    all_gather x15 -> x0, blocking collectives: 31.3 us -> none  [advance(): full_rows = lax.all_gather(current, 'mp', axis=2, tiled=True)]
  transfers between devices with their start and end apart: 35 -> 2, of which waited for: 34 -> 1; matrix products, arithmetic and copies ran while one was open for 4% -> 4% of each run, Pallas kernels for 0% -> 83%
where the time goes in v1:
time: 290 us; the launch traced here: 288 us
  Pallas kernels  239 us (82%)
  blocking collectives  14.7 us (5%)
  starting transfers between devices  14.1 us (5%)
  local copies, waits for them, and re-layouts  11.2 us (4%)
  waiting for transfers between devices  5.25 us (2%)
  other arithmetic  3.58 us (1%)
    pallas_call x1, Pallas kernels, per_device(): pl.pallas_call(layer_pipeline, out_shape=jax.ShapeDtypeStruct((FILES_N, 1...  239 us
    all_to_all x1, blocking collectives, per_device(): lax.all_to_all(slots, 'section', split_axis=0, concat_axis=0, tiled=True)  14.7 us
    all_to_all x1, starting transfers between devices, per_device(): lax.all_to_all(filled, 'dp', split_axis=0, concat_axis=0, tiled=True)  7.42 us
    all_to_all x1, starting transfers between devices, per_device(): lax.all_to_all(outgoing, 'dp', split_axis=0, concat_axis=0, tiled=True)  6.65 us
  transfers between devices with their start and end apart: 2, of which 1 were waited for; matrix products, arithmetic and copies ran while one was open for 4% of the time, Pallas kernels for 83%

profile of v1, /device:TPU:6, one launch (start us, length us, event | category | flops | bytes accessed | tf_op | source)
XLA Modules:
  0.0 288.1 jit_solution(18006767521427896440)
XLA Ops:
  0.0 0.7 iota_compare_fusion.2
  0.7 0.9 convert_reduce_fusion.1
  1.7 0.7 copy.23
  2.4 7.4 %all-to-all-start = ((s32[16,1,2]{2,1,0:T(1,128)}), s32[16,1,2]{2,1,0:T(1,128)S(1)}, u32[]{:S(2)}, u32[]{:S(2)}) async-start(s32[16,1,2]{2,1,0:T(1,128)} %copy.23), calls=%async_computation | async-start | bytes 16384 | tf_op jit(solution)/shard_map/all_to_all | solution.py:375
  9.9 0.7 fusion.8
  10.6 0.7 lt.55
  11.3 2.8 copy.30
  14.4 0.6 broadcast_bitcast_fusion.keyok
  15.2 0.6 tile.8
  15.9 0.6 tile.20
  16.5 0.8 broadcast_in_dim.5.rowok
  17.2 238.7 %layers.1 = bf16[8,16,384]{2,1,0:T(8,128)(2,1)} custom-call(bf16[256,1536]{1,0:T(8,128)(2,1)} %bitcast.19, bf16[192,1536]{1,0:T(8,128)(2,1)} %bitcast.20, bf16[192,1536]{1,0:T(8,128)(2,1)} %bitcast.21, bf16[3072,256]{1,0:T(8,128)(2,1)} %bitcast.16, f32[1,3072]{1,0:T(1,128)} %gain.1, f32[1,3072]{1,0:T(1,128)} %bias.1, f32[64,128]{1,0:T(8,128)} %bitcast.22, ...), custom_call_target="tpu_custom_call" | custom-call | tf_op jit(solution)/shard_map/layers/pallas_call | solution.py:394
  255.9 0.9 reshape.203
  256.9 0.4 fusion.4
  257.2 1.1 copy.25
  258.4 6.6 %all-to-all-start.1 = ((bf16[16,2,6144]{2,1,0:T(2,128)(2,1)}), bf16[16,2,6144]{2,1,0:T(2,128)(2,1)S(1)}, u32[]{:S(2)}, u32[]{:S(2)}) async-start(bf16[16,2,6144]{2,1,0:T(2,128)(2,1)} %copy.25), calls=%async_computation.1 | async-start | bytes 786432 | tf_op jit(solution)/shard_map/all_to_all | solution.py:446
  265.1 0.5 broadcast.110
  265.6 0.7 reduce.7
  266.6 5.2 %all-to-all-done.1 = bf16[16,2,6144]{2,1,0:T(2,128)(2,1)S(1)} async-done(((bf16[16,2,6144]{2,1,0:T(2,128)(2,1)}), bf16[16,2,6144]{2,1,0:T(2,128)(2,1)S(1)}, u32[]{:S(2)}, u32[]{:S(2)}) %all-to-all-start.1) | async-done | bytes 393248 | tf_op jit(solution)/shard_map/all_to_all | solution.py:446
  271.9 0.1 reshape.204
  272.0 0.2 fusion
  272.3 0.2 copy.26
  272.5 14.7 %all_to_all.19 = bf16[8,2,6144]{2,1,0:T(2,128)(2,1)S(1)} all-to-all(bf16[8,2,6144]{2,1,0:T(2,128)(2,1)S(1)} %copy.26), channel_id=1, replica_groups=mesh['dp'=16,'section'=8,'mp'=2] {'section'}, dimensions={0} | all-to-all | bytes 393216 | tf_op jit(solution)/shard_map/all_to_all | solution.py:450
  287.4 0.8 reshape.201
  (21 shorter events, 1.3 us)
Async XLA Ops:
  2.4 256.0 %all-to-all-start = ((s32[16,1,2]{2,1,0:T(1,128)}), s32[16,1,2]{2,1,0:T(1,128)S(1)}, u32[]{:S(2)}, u32[]{:S(2)}) async-start(s32[16,1,2]{2,1,0:T(1,128)} %copy.23), calls=%async_computation | async-start | bytes 16384 | tf_op jit(solution)/shard_map/all_to_all | solution.py:375
  258.4 13.5 %all-to-all-start.1 = ((bf16[16,2,6144]{2,1,0:T(2,128)(2,1)}), bf16[16,2,6144]{2,1,0:T(2,128)(2,1)S(1)}, u32[]{:S(2)}, u32[]{:S(2)}) async-start(bf16[16,2,6144]{2,1,0:T(2,128)(2,1)} %copy.25), calls=%async_computation.1 | async-start | bytes 786432 | tf_op jit(solution)/shard_map/all_to_all | solution.py:446

commit v2 on v1

v2 whole, which is shorter than its diff:
```python
import jax
import jax.numpy as jnp
import numpy as np
from jax import lax
from jax.experimental import pallas as pl
from jax.experimental.pallas import tpu as pltpu
from jax.sharding import PartitionSpec as P

GSLOTS = 16
MESH = pl.DeviceIdType.MESH

rope_base = 100000.0
norm_eps = 1e-05

FILES_N = 8
LEN = 32
ROWS = FILES_N * LEN
WIDTH = 3072
HALF = 1536
SHARD = 192
PART = 48
HEAD = 128
GROUP = 12
MICRO = 64
MICROS = ROWS // MICRO
MFILES = MICRO // LEN
SECTIONS = 8
SIDE = 4
CUT = 384
CHUNK = 512
CHUNKS = HALF // CHUNK
PLANE = SIDE * SIDE


def rope_tables(length_n, head_size):
    position = np.arange(length_n, dtype=np.float32)
    fraction = np.arange(head_size // 2, dtype=np.float32) * np.float32(2.0 / head_size)
    inverse = np.power(np.float32(rope_base), -fraction)
    angles = position[:, None] * inverse[None, :]
    cosine, sine = np.cos(angles), np.sin(angles)
    return (
        np.concatenate([cosine, cosine], axis=-1),
        np.concatenate([-sine, sine], axis=-1),
    )


def layer_pipeline(
    hidden, wq_own, wo_own, wkv_hbm, gain, bias, cosine, sine, dest_wide, dest_own, lengths, out,
    wq, wo, wkv, wot, stream, psend, precv, updated, final, piece, normed, queries, context,
    dest_all, outgoing, arrived_files, slots, landed, dest_s, slot_s,
    local_sem, gsend, grecv, zsend, zrecv, asend, arecv, rsend, rrecv, ssend, srecv,
    isend, irecv, fsend, frecv, osend, orecv,
):
    dp = lax.axis_index("dp")
    section = lax.axis_index("section")
    core = lax.axis_index("mp")
    x = lax.rem(dp, SIDE)
    y = dp // SIDE

    def at_xy(xx, yy):
        return lax.rem(yy + SIDE, SIDE) * SIDE + lax.rem(xx + SIDE, SIDE)

    other = 1 - core
    partner = (dp, section, other)
    steps = ((1, 0), (-1, 0), (0, 1), (0, -1))

    barrier = pltpu.get_barrier_semaphore()

    def greet(k, carry):
        pl.semaphore_signal(
            barrier,
            inc=1,
            device_id=(lax.rem(dp + k, PLANE), section, core),
            device_id_type=MESH,
        )
        return carry

    lax.fori_loop(1, PLANE, greet, 0)
    pl.semaphore_signal(barrier, inc=1, device_id=partner, device_id_type=MESH)
    for k in range(1, SECTIONS):
        pl.semaphore_signal(
            barrier, inc=1, device_id=(dp, lax.rem(section + k, SECTIONS), core), device_id_type=MESH
        )
    pl.semaphore_wait(barrier, PLANE - 1 + 1 + SECTIONS - 1)

    own_cols = pl.ds(pl.multiple_of(core * HALF, HALF), HALF)

    copies = [
        pltpu.make_async_copy(wq_own, wq.at[pl.ds(pl.multiple_of(dp * SHARD, SHARD), SHARD), :], local_sem.at[0]),
        pltpu.make_async_copy(wo_own, wo.at[pl.ds(pl.multiple_of(dp * SHARD, SHARD), SHARD), :], local_sem.at[1]),
        pltpu.make_async_copy(wkv_hbm, wkv, local_sem.at[2]),
    ]
    for copy in copies:
        copy.start()

    def rows_of(source, part):
        return pl.ds(pl.multiple_of(source * SHARD + part * PART, PART), PART)

    def push(w, source, part, direction, own):
        full = (wq, wo)[w]
        sx, sy = steps[direction]
        place = full.at[rows_of(source, part), :]
        src = (wq_own, wo_own)[w].at[pl.ds(part * PART, PART), :] if own else place
        pltpu.make_async_remote_copy(
            src_ref=src,
            dst_ref=place,
            send_sem=gsend.at[w, direction],
            recv_sem=grecv.at[w, source, part],
            device_id=(at_xy(x + sx, y + sy), section, core),
            device_id_type=MESH,
        ).start()

    def arrived(w, source, part):
        place = (wq, wo)[w].at[rows_of(source, part), :]
        pltpu.make_async_copy(place, place, grecv.at[w, source, part]).wait()

    def first_dirs(colour):
        return (0, 1) if colour == 0 else (2, 3)

    def second_dirs(colour):
        return (2, 3) if colour == 0 else (0, 1)

    def along(colour, k):
        return at_xy(x + k, y) if colour == 0 else at_xy(x, y + k)

    def across(colour, k, j):
        return at_xy(x + k, y + j) if colour == 0 else at_xy(x + j, y + k)

    def spread_own(w):
        for dirs in (first_dirs, second_dirs):
            for part in range(2):
                for colour in range(2):
                    for direction in dirs(colour):
                        push(w, dp, 2 * colour + part, direction, True)

    def relay_first(w):
        for part in range(2):
            for colour in range(2):
                forward, backward = first_dirs(colour)
                arrived(w, along(colour, -1), 2 * colour + part)
                if part == 0:
                    push(w, along(colour, -1), 2 * colour, forward, False)
                arrived(w, along(colour, 1), 2 * colour + part)
                if part == 1:
                    push(w, along(colour, 1), 2 * colour + 1, backward, False)
        for k in (-1, 1):
            for part in range(2):
                for colour in range(2):
                    for direction in second_dirs(colour):
                        push(w, along(colour, k), 2 * colour + part, direction, False)

    def relay_opposite(w):
        for part in range(2):
            for colour in range(2):
                arrived(w, along(colour, 2), 2 * colour + part)
                for direction in second_dirs(colour):
                    push(w, along(colour, 2), 2 * colour + part, direction, False)

    def relay_second(w, k):
        for part in range(2):
            for colour in range(2):
                forward, backward = second_dirs(colour)
                arrived(w, across(colour, k, -1), 2 * colour + part)
                if part == 0:
                    push(w, across(colour, k, -1), 2 * colour, forward, False)
                arrived(w, across(colour, k, 1), 2 * colour + part)
                if part == 1:
                    push(w, across(colour, k, 1), 2 * colour + 1, backward, False)

    def finish(w):
        for k in (0, -1, 1, 2):
            for part in range(2):
                for colour in range(2):
                    arrived(w, across(colour, k, 2), 2 * colour + part)

    def micro_rows(i):
        return pl.ds(pl.multiple_of(i * MICRO, MICRO), MICRO)

    def chunk_cols(j):
        return pl.ds(pl.multiple_of(core * HALF + j * CHUNK, CHUNK), CHUNK)

    def half_chunk(j):
        return pl.ds(j * CHUNK, CHUNK)

    def hop(i, j, to_section):
        rows = micro_rows(i)
        return pltpu.make_async_remote_copy(
            src_ref=updated.at[rows, half_chunk(j)],
            dst_ref=stream.at[rows, chunk_cols(j)],
            send_sem=zsend.at[i, j],
            recv_sem=zrecv.at[i, j],
            device_id=(dp, to_section, core),
            device_id_type=MESH,
        )

    def swap(i, j):
        rows = micro_rows(i)
        return pltpu.make_async_remote_copy(
            src_ref=stream.at[rows, chunk_cols(j)],
            dst_ref=stream.at[rows, chunk_cols(j)],
            send_sem=asend.at[i, j],
            recv_sem=arecv.at[i, j],
            device_id=partner,
            device_id_type=MESH,
        )

    def give(i, j):
        rows = micro_rows(i)
        return pltpu.make_async_remote_copy(
            src_ref=psend.at[rows, half_chunk(j)],
            dst_ref=precv.at[rows, half_chunk(j)],
            send_sem=rsend.at[i, j],
            recv_sem=rrecv.at[i, j],
            device_id=partner,
            device_id_type=MESH,
        )

    def spread(i, target):
        files = pl.ds(i * MFILES, MFILES)
        return (
            final.at[files, target // 4, :, pl.ds((target % 4) * CUT, CUT)],
            piece.at[files, :, :],
        )

    row_id = lax.broadcasted_iota(jnp.int32, (MICRO, MICRO), 0)
    col_id = lax.broadcasted_iota(jnp.int32, (MICRO, MICRO), 1)
    causal = (row_id // LEN == col_id // LEN) & (col_id <= row_id)
    score_scale = HEAD ** (-0.5)

    def inside(ids, i):
        limit = jnp.zeros_like(ids)
        for f in range(MFILES):
            limit = jnp.where(ids // LEN == f, lengths[i * MFILES + f] + f * LEN, limit)
        return ids < limit

    def attend(i):
        rows = micro_rows(i)
        for block in range(MICRO // 16):
            part = pl.ds(pl.multiple_of(i * MICRO + block * 16, 16), 16)
            values = stream[part, :].astype(jnp.float32)
            center = jnp.mean(values, axis=-1, keepdims=True)
            values = values - center
            variance = jnp.mean(values * values, axis=-1, keepdims=True)
            scaled = values * lax.rsqrt(variance + norm_eps)
            normed[block * 16 : (block + 1) * 16, :] = (scaled * gain[...] + bias[...]).astype(
                jnp.bfloat16
            )

        cos_t = cosine[...]
        sin_t = sine[...]

        def rotate(values):
            return values * cos_t + pltpu.roll(values, HEAD // 2, 1) * sin_t

        keyval = jnp.dot(normed[...], wkv[...], preferred_element_type=jnp.float32)
        key = rotate(keyval[:, :HEAD]).astype(jnp.bfloat16)
        value = keyval[:, HEAD:].astype(jnp.bfloat16)
        for j in range(GROUP // 2):
            pair = jnp.dot(
                normed[...], wq[:, j * 256 : (j + 1) * 256], preferred_element_type=jnp.float32
            )
            for k in range(2):
                h = 2 * j + k
                queries[h * MICRO : (h + 1) * MICRO, :] = rotate(
                    pair[:, k * HEAD : (k + 1) * HEAD]
                ).astype(jnp.bfloat16)
        scores = lax.dot_general(
            queries[...], key, (((1,), (1,)), ((), ())), preferred_element_type=jnp.float32
        )
        ok = causal & inside(col_id, i)
        scores = (scores * score_scale).reshape(GROUP, MICRO, MICRO)
        scores = jnp.where(ok[None], scores, -jnp.inf)
        highest = jnp.max(scores, axis=-1, keepdims=True)
        weights = jnp.exp(scores - highest)
        total = jnp.sum(weights, axis=-1, keepdims=True)
        probs = (weights / total).astype(jnp.bfloat16).reshape(GROUP * MICRO, MICRO)
        mixed = jnp.dot(probs, value, preferred_element_type=jnp.float32).astype(jnp.bfloat16)
        for h in range(GROUP):
            context[rows, h * HEAD : (h + 1) * HEAD] = mixed[h * MICRO : (h + 1) * MICRO, :]

    def project(i, half, j, turned):
        start = pl.multiple_of(half * HALF + j * 256, 256)
        if turned:
            return jnp.dot(
                context[micro_rows(i), :],
                wot[:, pl.ds(start, 256)],
                preferred_element_type=jnp.float32,
            ).astype(jnp.bfloat16)
        return lax.dot_general(
            context[micro_rows(i), :],
            wo[pl.ds(start, 256), :],
            (((1,), (1,)), ((), ())),
            preferred_element_type=jnp.float32,
        ).astype(jnp.bfloat16)

    def output(i, turned, last):
        rows = micro_rows(i)

        def others(c):
            for j in range(c * CHUNK // 256, (c + 1) * CHUNK // 256):
                psend[rows, j * 256 : (j + 1) * 256] = project(i, other, j, turned)
            give(i, c).start()

        def mine(c):
            for j in range(c * CHUNK // 256, (c + 1) * CHUNK // 256):
                updated[rows, j * 256 : (j + 1) * 256] = project(i, core, j, turned)

        def join(c):
            give(i, c).wait_recv()
            cols = half_chunk(c)
            total = updated[rows, cols].astype(jnp.float32) + precv[rows, cols].astype(jnp.float32)
            result = (stream[rows, chunk_cols(c)].astype(jnp.float32) + total).astype(jnp.bfloat16)
            updated[rows, cols] = result
            hop_on(c, result)

        def hop_on(c, result):
            if last is None:
                hop(i, c, section + 1).start()
            else:
                last(i, c, result)

        others(0)
        others(1)
        mine(0)
        others(2)
        join(0)
        mine(1)
        join(1)
        mine(2)
        join(2)

    def hold(i, c, result):
        @pl.when(section < SECTIONS - 1)
        def _():
            hop(i, c, section + 1).start()

        @pl.when(section == SECTIONS - 1)
        def _():
            kept = jnp.where(inside(row_id[:, 0:1], i), result, jnp.zeros_like(result))
            final[pl.ds(i * MFILES, MFILES), :, :, c * CHUNK : (c + 1) * CHUNK] = kept.reshape(
                MFILES, 2, 16, CHUNK
            )

    spread_own(0)

    dest_all[dp] = dest_wide[...]

    def tell(k, carry):
        to = lax.rem(dp + k, PLANE)
        pltpu.make_async_remote_copy(
            src_ref=dest_wide,
            dst_ref=dest_all.at[dp],
            send_sem=isend.at[0],
            recv_sem=irecv.at[0],
            device_id=(to, section, core),
            device_id_type=MESH,
        ).start()
        return carry

    lax.fori_loop(1, PLANE, tell, 0)

    @pl.when(section == 0)
    def _():
        first = pltpu.make_async_copy(hidden, stream.at[:, own_cols], local_sem.at[3])
        first.start()
        first.wait()

        def begin(i, carry):
            for j in range(CHUNKS):
                swap(i, j).start()
            return carry

        lax.fori_loop(0, MICROS, begin, 0)

    relay_first(0)
    spread_own(1)

    told = dest_all.at[pl.ds(0, PLANE - 1)]
    pltpu.make_async_copy(told, told, isend.at[0]).wait()
    pltpu.make_async_copy(told, told, irecv.at[0]).wait()
    lift = pltpu.make_async_copy(dest_all, dest_s, local_sem.at[4])
    lift.start()

    relay_opposite(0)
    relay_second(0, 0)
    lift.wait()

    def rank(source, carry):
        count, places = carry
        own_count = jnp.int32(0)
        for f in range(FILES_N):
            hit = dest_s[source, f, 0] == dp
            spot = source * 2 + own_count
            places = tuple(
                jnp.where(hit & (count == k), spot, places[k]) for k in range(GSLOTS)
            )
            step_up = jnp.where(hit, 1, 0)
            count = count + step_up
            own_count = own_count + step_up
        return count, places

    count, places = lax.fori_loop(0, PLANE, rank, (jnp.int32(0), (jnp.int32(0),) * GSLOTS))
    for k in range(GSLOTS):
        slot_s[k] = places[k]
    slot_s[GSLOTS] = count

    relay_first(1)
    relay_second(0, -1)
    relay_second(0, 1)
    relay_opposite(1)
    relay_second(0, 2)
    finish(0)
    for copy in copies:
        copy.wait()

    def relay_and_attend(t, carry):
        relay_second(1, jnp.where(t < 2, t, 5 - t))

        @pl.when(section == 0)
        def _():
            for j in range(CHUNKS):
                swap(t, j).wait_recv()
            attend(t)

        return carry

    lax.fori_loop(0, MICROS, relay_and_attend, 0)
    finish(1)

    @pl.when(section > 0)
    def _():
        def turn(j, carry):
            start = pl.multiple_of(j * 256, 256)
            wot[:, pl.ds(start, 256)] = wo[pl.ds(start, 256), :].T
            return carry

        lax.fori_loop(0, WIDTH // 256, turn, 0)

    def step(i, carry):
        @pl.when(section == 0)
        def _():
            output(i, False, None)

        @pl.when(section > 0)
        def _():
            for j in range(CHUNKS):
                hop(i, j, section).wait_recv()
                swap(i, j).start()
            for j in range(CHUNKS):
                swap(i, j).wait_recv()
            attend(i)
            output(i, True, hold)

        @pl.when(section == SECTIONS - 1)
        def _():
            for target in range(SECTIONS - 1):
                src, dst = spread(i, target)
                pltpu.make_async_remote_copy(
                    src_ref=src,
                    dst_ref=dst,
                    send_sem=ssend.at[i, target],
                    recv_sem=srecv.at[i],
                    device_id=(dp, target, core),
                    device_id_type=MESH,
                ).start()
            src, dst = spread(i, SECTIONS - 1)
            pltpu.make_async_copy(src, dst, srecv.at[i]).start()

        return carry

    lax.fori_loop(0, MICROS, step, 0)

    def gathered(i, carry):
        files = piece.at[pl.ds(i * MFILES, MFILES), :, :]
        pltpu.make_async_copy(files, files, srecv.at[i]).wait()
        return carry

    lax.fori_loop(0, MICROS, gathered, 0)

    def post(k, carry):
        to = lax.rem(dp + k, PLANE)
        picks = [jnp.int32(0), jnp.int32(0)]
        seen = jnp.int32(0)
        for f in range(FILES_N):
            hit = dest_own[f] == to
            for n in range(2):
                picks[n] = jnp.where(hit & (seen == n), f, picks[n])
            seen = seen + jnp.where(hit, 1, 0)
        for n in range(2):
            outgoing[2 * k + n] = piece[picks[n]]
        pair = outgoing.at[pl.ds(2 * k, 2)]
        land = arrived_files.at[pl.ds(2 * dp, 2)]

        @pl.when(k > 0)
        def _():
            pltpu.make_async_remote_copy(
                src_ref=pair,
                dst_ref=land,
                send_sem=fsend.at[0],
                recv_sem=frecv.at[0],
                device_id=(to, section, core),
                device_id_type=MESH,
            ).start()

        return carry

    lax.fori_loop(0, PLANE, post, 0)
    own_pair = pltpu.make_async_copy(
        outgoing.at[pl.ds(0, 2)], arrived_files.at[pl.ds(2 * dp, 2)], local_sem.at[5]
    )
    own_pair.start()
    own_pair.wait()
    posted = outgoing.at[pl.ds(0, 2 * (PLANE - 1))]
    pltpu.make_async_copy(posted, posted, frecv.at[0]).wait()

    for k in range(GSLOTS):
        block = arrived_files[slot_s[k]]
        slots[k] = jnp.where(k < slot_s[GSLOTS], block, jnp.zeros_like(block))

    def landing():
        return landed.at[:, section // 4, :, pl.ds(pl.multiple_of((section % 4) * CUT, CUT), CUT)]

    def deliver(k, carry):
        to = lax.rem(section + k, SECTIONS)
        pltpu.make_async_remote_copy(
            src_ref=slots.at[pl.ds(2 * to, 2)],
            dst_ref=landing(),
            send_sem=osend.at[0],
            recv_sem=orecv.at[0],
            device_id=(dp, to, core),
            device_id_type=MESH,
        ).start()
        return carry

    lax.fori_loop(1, SECTIONS, deliver, 0)
    own_slots = pltpu.make_async_copy(slots.at[pl.ds(2 * section, 2)], landing(), local_sem.at[5])
    own_slots.start()
    own_slots.wait()
    delivered = slots.at[pl.ds(0, 2 * (SECTIONS - 1))]
    pltpu.make_async_copy(delivered, delivered, orecv.at[0]).wait()
    out[...] = landed[...]

    def drain(i, carry):
        for j in range(CHUNKS):
            swap(i, j).wait_send()
            give(i, j).wait_send()

        @pl.when(section < SECTIONS - 1)
        def _():
            for j in range(CHUNKS):
                hop(i, j, section).wait_send()

        @pl.when(section == SECTIONS - 1)
        def _():
            for target in range(SECTIONS - 1):
                src, dst = spread(i, target)
                pltpu.make_async_copy(src, dst, ssend.at[i, target]).wait()

        return carry

    lax.fori_loop(0, MICROS, drain, 0)
    for w in range(2):
        for direction in range(4):
            sent = (wq, wo)[w].at[pl.ds(0, 15 * PART), :]
            pltpu.make_async_copy(sent, sent, gsend.at[w, direction]).wait()
    pltpu.make_async_copy(posted, posted, fsend.at[0]).wait()
    pltpu.make_async_copy(delivered, delivered, osend.at[0]).wait()


def per_device(hidden, lengths, dest_group, w_query, w_keyval, w_output, norm_gain, norm_bias):
    source_files, length_n, half_width = hidden.shape
    cosine, sine = rope_tables(length_n, HEAD)
    cosine, sine = jnp.asarray(np.tile(cosine, (MFILES, 1))), jnp.asarray(np.tile(sine, (MFILES, 1)))
    dest_wide = jnp.broadcast_to(dest_group[:, None], (source_files, 128))

    anywhere = pl.BlockSpec(memory_space=pl.ANY)
    inner = pl.BlockSpec(memory_space=pltpu.VMEM)
    scalar = pl.BlockSpec(memory_space=pltpu.SMEM)
    dma = pltpu.SemaphoreType.DMA
    bf16 = jnp.bfloat16
    rows = pl.pallas_call(
        layer_pipeline,
        out_shape=jax.ShapeDtypeStruct((2, 2, 16, HALF), bf16),
        in_specs=[anywhere] * 4 + [inner] * 5 + [scalar] * 2,
        out_specs=inner,
        scratch_shapes=[
            pltpu.VMEM((WIDTH, HALF), bf16),
            pltpu.VMEM((WIDTH, HALF), bf16),
            pltpu.VMEM((WIDTH, 2 * HEAD), bf16),
            pltpu.VMEM((HALF, WIDTH), bf16),
            pltpu.VMEM((ROWS, WIDTH), bf16),
            pltpu.VMEM((ROWS, HALF), bf16),
            pltpu.VMEM((ROWS, HALF), bf16),
            pltpu.VMEM((ROWS, HALF), bf16),
            pltpu.VMEM((FILES_N, 2, 16, HALF), bf16),
            pltpu.VMEM((FILES_N, 16, CUT), bf16),
            pltpu.VMEM((MICRO, WIDTH), bf16),
            pltpu.VMEM((GROUP * MICRO, HEAD), bf16),
            pltpu.VMEM((ROWS, HALF), bf16),
            pltpu.VMEM((PLANE, FILES_N, 128), jnp.int32),
            pltpu.VMEM((2 * PLANE, 16, CUT), bf16),
            pltpu.VMEM((2 * PLANE, 16, CUT), bf16),
            pltpu.VMEM((GSLOTS, 16, CUT), bf16),
            pltpu.VMEM((2, 2, 16, HALF), bf16),
            pltpu.SMEM((PLANE, FILES_N, 128), jnp.int32),
            pltpu.SMEM((GSLOTS + 1,), jnp.int32),
            dma((6,)),
            dma((2, 4)),
            dma((2, 16, 4)),
            dma((MICROS, CHUNKS)),
            dma((MICROS, CHUNKS)),
            dma((MICROS, CHUNKS)),
            dma((MICROS, CHUNKS)),
            dma((MICROS, CHUNKS)),
            dma((MICROS, CHUNKS)),
            dma((MICROS, SECTIONS)),
            dma((MICROS,)),
            dma((1,)),
            dma((1,)),
            dma((1,)),
            dma((1,)),
            dma((1,)),
            dma((1,)),
        ],
        compiler_params=pltpu.CompilerParams(
            collective_id=0, has_side_effects=True, vmem_limit_bytes=58 * 2**20
        ),
        name="layers",
    )(
        hidden.reshape(ROWS, HALF),
        w_query[0],
        w_output[0],
        w_keyval[0].reshape(WIDTH, 2 * HEAD),
        norm_gain,
        norm_bias,
        cosine,
        sine,
        dest_wide,
        dest_group,
        lengths,
    )
    return rows.reshape(GSLOTS // SECTIONS, length_n, half_width)


def solution(mesh):
    in_specs = (
        P("dp", None, "mp"),
        P("dp"),
        P("dp"),
        P("section", "dp", "mp"),
        P("section", None, "mp", None, None),
        P("section", "dp", "mp"),
        P("section", None),
        P("section", None),
    )
    out_specs = P(("dp", "section"), None, "mp")
    return jax.shard_map(
        per_device, mesh=mesh, in_specs=in_specs, out_specs=out_specs, check_vma=False
    )
```

time: 290 us -> 242 us (0.83)
  blocking collectives: 14.7 us -> 0 us
  starting transfers between devices: 14.1 us -> 0 us
  local copies, waits for them, and re-layouts: 11.2 us -> 5.7 us
  waiting for transfers between devices: 5.25 us -> 0 us
  Pallas kernels: 239 us -> 235 us
  other arithmetic: 3.58 us -> 0 us
    all_to_all x1 -> x0, blocking collectives: 14.7 us -> none  [per_device(): lax.all_to_all(slots, 'section', split_axis=0, concat_axis=0, tiled=True)]
    all_to_all x2 -> x0, starting transfers between devices: 14.1 us -> none  [the longest x1 7.42 us: per_device(): lax.all_to_all(filled, 'dp', split_axis=0, concat_axis=0, tiled=True)]
    all_to_all x2 -> x0, waiting for transfers between devices: 5.25 us -> none  [the longest x1 5.25 us: per_device(): lax.all_to_all(outgoing, 'dp', split_axis=0, concat_axis=0, tiled=True)]
    pallas_call x1, Pallas kernels: 239 us -> 235 us  [per_device(): pl.pallas_call(layer_pipeline, out_shape=jax.ShapeDtypeStruct((2, 2, 16,...]
  transfers between devices with their start and end apart: 2 -> 0, of which waited for: 1 -> 0; matrix products, arithmetic and copies ran while one was open for 4% -> 0% of each run, Pallas kernels for 83% -> 0%
where the time goes in v2:
time: 242 us; the launch traced here: 241 us
  Pallas kernels  235 us (97%)
  local copies, waits for them, and re-layouts  5.7 us (2%)
    pallas_call x1, Pallas kernels, per_device(): pl.pallas_call(layer_pipeline, out_shape=jax.ShapeDtypeStruct((2, 2, 16,...  235 us

profile of v2, /device:TPU:6, one launch (start us, length us, event | category | flops | bytes accessed | tf_op | source)
XLA Modules:
  0.0 241.1 jit_solution(15257262961506489407)
XLA Ops:
  0.0 1.3 broadcast_in_dim.2.dest_wide
  1.3 2.8 %copy.13 = bf16[384,8,2,128]{3,1,2,0:T(8,128)(2,1)} copy(bf16[384,8,2,128]{3,2,1,0:T(2,128)(2,1)} %bitcast.10) | data formatting | bytes 3145728
  4.1 235.4 %layers.1 = bf16[2,2,16,1536]{3,2,1,0:T(8,128)(2,1)} custom-call(bf16[256,1536]{1,0:T(8,128)(2,1)} %bitcast.12, bf16[192,1536]{1,0:T(8,128)(2,1)} %bitcast.13, bf16[192,1536]{1,0:T(8,128)(2,1)} %bitcast.14, bf16[3072,256]{1,0:T(8,128)(2,1)} %bitcast.9, f32[1,3072]{1,0:T(1,128)} %gain.1, f32[1,3072]{1,0:T(1,128)} %bias.1, f32[64,128]{1,0:T(8,128)} %constant.4.clone.cosine, ...), custom_call_target="tpu_custom_call" | custom-call | tf_op jit(solution)/shard_map/layers/pallas_call | solution.py:581
  239.5 1.6 copy.15

commit v3 on v2

--- a/solution.py
+++ b/solution.py
@@ -293,8 +293,20 @@
             preferred_element_type=jnp.float32,
         ).astype(jnp.bfloat16)
 
+    def fetch(i, j):
+        hop(i, j, section).wait_recv()
+        swap(i, j).start()
+
     def output(i, turned, last):
         rows = micro_rows(i)
+
+        def ahead(chunks):
+            if last is not None:
+
+                @pl.when(i < MICROS - 1)
+                def _():
+                    for j in chunks:
+                        fetch(i + 1, j)
 
         def others(c):
             for j in range(c * CHUNK // 256, (c + 1) * CHUNK // 256):
@@ -327,7 +339,9 @@
         mine(1)
         join(1)
         mine(2)
+        ahead((0, 1))
         join(2)
+        ahead((2,))
 
     def hold(i, c, result):
         @pl.when(section < SECTIONS - 1)
@@ -418,13 +432,17 @@
 
         @pl.when(section == 0)
         def _():
-            for j in range(CHUNKS):
-                swap(t, j).wait_recv()
-            attend(t)
-
-        return carry
-
-    lax.fori_loop(0, MICROS, relay_and_attend, 0)
+            def early(i, inner):
+                for j in range(CHUNKS):
+                    swap(i, j).wait_recv()
+                attend(i)
+                return inner
+
+            lax.fori_loop(t * (MICROS // SIDE), (t + 1) * (MICROS // SIDE), early, 0)
+
+        return carry
+
+    lax.fori_loop(0, SIDE, relay_and_attend, 0)
     finish(1)
 
     @pl.when(section > 0)
@@ -435,6 +453,8 @@
             return carry
 
         lax.fori_loop(0, WIDTH // 256, turn, 0)
+        for j in range(CHUNKS):
+            fetch(0, j)
 
     def step(i, carry):
         @pl.when(section == 0)
@@ -443,9 +463,6 @@
 
         @pl.when(section > 0)
         def _():
-            for j in range(CHUNKS):
-                hop(i, j, section).wait_recv()
-                swap(i, j).start()
             for j in range(CHUNKS):
                 swap(i, j).wait_recv()
             attend(i)

time: 242 us -> 241 us (level)
  no operation moved by 1% of the time
where the time goes in v3:
time: 241 us
  Pallas kernels  235 us (98%)
  local copies, waits for them, and re-layouts  5.7 us (2%)
    pallas_call x1, Pallas kernels, per_device(): pl.pallas_call(layer_pipeline, out_shape=jax.ShapeDtypeStruct((2, 2, 16,...  235 us

profile of v3, /device:TPU:6, one launch (start us, length us, event | category | flops | bytes accessed | tf_op | source)
XLA Modules:
  0.0 240.7 jit_solution(13980500871346379114)
XLA Ops:
  0.0 1.3 broadcast_in_dim.2.dest_wide
  1.3 2.8 %copy.13 = bf16[384,8,2,128]{3,1,2,0:T(8,128)(2,1)} copy(bf16[384,8,2,128]{3,2,1,0:T(2,128)(2,1)} %bitcast.10) | data formatting | bytes 3145728
  4.1 235.0 %layers.1 = bf16[2,2,16,1536]{3,2,1,0:T(8,128)(2,1)} custom-call(bf16[256,1536]{1,0:T(8,128)(2,1)} %bitcast.12, bf16[192,1536]{1,0:T(8,128)(2,1)} %bitcast.13, bf16[192,1536]{1,0:T(8,128)(2,1)} %bitcast.14, bf16[3072,256]{1,0:T(8,128)(2,1)} %bitcast.9, f32[1,3072]{1,0:T(1,128)} %gain.1, f32[1,3072]{1,0:T(1,128)} %bias.1, f32[64,128]{1,0:T(8,128)} %constant.4.clone.cosine, ...), custom_call_target="tpu_custom_call" | custom-call | tf_op jit(solution)/shard_map/layers/pallas_call | solution.py:598
  239.1 1.6 copy.15

commit v4 on v3

--- a/solution.py
+++ b/solution.py
@@ -21,7 +21,7 @@
 PART = 48
 HEAD = 128
 GROUP = 12
-MICRO = 64
+MICRO = 32
 MICROS = ROWS // MICRO
 MFILES = MICRO // LEN
 SECTIONS = 8

time: 241 us -> 258 us (1.071)
  Pallas kernels: 235 us -> 252 us
    pallas_call x1, Pallas kernels: 235 us -> 252 us  [per_device(): pl.pallas_call(layer_pipeline, out_shape=jax.ShapeDtypeStruct((2, 2, 16,...]
where the time goes in v4:
time: 258 us
  Pallas kernels  252 us (98%)
  local copies, waits for them, and re-layouts  5.7 us (2%)
    pallas_call x1, Pallas kernels, per_device(): pl.pallas_call(layer_pipeline, out_shape=jax.ShapeDtypeStruct((2, 2, 16,...  252 us

profile of v4, /device:TPU:6, one launch (start us, length us, event | category | flops | bytes accessed | tf_op | source)
XLA Modules:
  0.0 257.6 jit_solution(14573445126588963613)
XLA Ops:
  0.0 1.3 broadcast_in_dim.2.dest_wide
  1.3 2.8 %copy.13 = bf16[384,8,2,128]{3,1,2,0:T(8,128)(2,1)} copy(bf16[384,8,2,128]{3,2,1,0:T(2,128)(2,1)} %bitcast.10) | data formatting | bytes 3145728
  4.1 251.9 %layers.1 = bf16[2,2,16,1536]{3,2,1,0:T(8,128)(2,1)} custom-call(bf16[256,1536]{1,0:T(8,128)(2,1)} %bitcast.12, bf16[192,1536]{1,0:T(8,128)(2,1)} %bitcast.13, bf16[192,1536]{1,0:T(8,128)(2,1)} %bitcast.14, bf16[3072,256]{1,0:T(8,128)(2,1)} %bitcast.9, f32[1,3072]{1,0:T(1,128)} %gain.1, f32[1,3072]{1,0:T(1,128)} %bias.1, f32[32,128]{1,0:T(8,128)} %constant.4.clone.cosine, ...), custom_call_target="tpu_custom_call" | custom-call | tf_op jit(solution)/shard_map/layers/pallas_call | solution.py:598
  256.0 1.6 copy.15
